TPU v7x, 128 devices: a whole 4x4x4 slice. The times are simulated.
128 devices in a mesh: blk: 16 (over y, z), rep: 8 (over x, core).
Axes of the slice: x: 4, y: 4, z: 4, core: 2. Of those that a mesh axis runs over, the one named last changes fastest.
Arguments:
- dense: bfloat16 [131072, 1024], P(('blk', 'rep')), may hold values from -6 to 6
- labels: int32 [131072], P(('blk', 'rep')), may hold values 0 or 1
- tile_values: bfloat16 [16384, 64, 128], P(('blk', 'rep')), may hold values from -1.1953125 to 1.1953125
- tile_block: int32 [16384, 64], P(('blk', 'rep')), may hold values from 0 to 1023
- tile_example: int32 [16384, 64], P(('blk', 'rep')), may hold values from 0 to 1023
- tile_count: int32 [16384], P(('blk', 'rep')), may hold values from 16 to 64, as said below
- z_state: float32 [131072, 128], P(('blk', 'rep')), may hold values from -6 to 6
- n_state: float32 [131072, 128], P(('blk', 'rep')), may hold values from 0.01 to 4
- w_one: bfloat16 [1024, 512], replicated, may hold values from -0.1875 to 0.1875
- b_one: float32 [512], replicated, may hold values from -3 to 3
- w_two: bfloat16 [512, 256], replicated, may hold values from -0.25 to 0.25
- b_two: float32 [256], replicated, may hold values from -3 to 3
- head: bfloat16 [256], replicated, may hold values from -0.375 to 0.375
Outputs:
- probability: float32 [131072], P(('blk', 'rep'))
- z_new: float32 [131072, 128], P(('blk', 'rep'))
- n_new: float32 [131072, 128], P(('blk', 'rep'))
- grad_w_one: float32 [1024, 512], replicated
- grad_b_one: float32 [512], replicated
- grad_w_two: float32 [512, 256], replicated
- grad_b_two: float32 [256], replicated
- grad_head: float32 [256], replicated
Inputs may be any that keep to these rules, and one draw needn't show every extreme that they name: `tile_count`: slots at or beyond a list's count are padding; in every draw some owners receive 64 live slots from every device.
All inputs are finite; a program needn't handle non-finite values. No bound on the sum of `labels` on one device may be relied on, other than what follows from the above.
Results may differ from a plain program's by a relative error of at most 0.013.
Values may be sent and summed in bfloat16 or wider, within the bound.
A program may use at most 64 MiB of HBM per device.

v0:
```python
import jax
import jax.numpy as jnp
from jax import lax
from jax.sharding import PartitionSpec as P

alpha_rate = 0.5
beta_shift = 1.0
lasso_term = 0.5
ridge_term = 0.1


def wide_weight(z_state, n_state):
    shrunk = z_state - jnp.sign(z_state) * lasso_term
    denominator = (beta_shift + jnp.sqrt(n_state)) / alpha_rate + ridge_term
    return jnp.where(jnp.abs(z_state) > lasso_term, -shrunk / denominator, jnp.zeros_like(z_state))


def silu_slope(pre):
    gate = jax.nn.sigmoid(pre)
    return gate * (1.0 + pre * (1.0 - gate))


def per_device(
    dense,
    labels,
    tile_values,
    tile_block,
    tile_example,
    tile_count,
    z_state,
    n_state,
    w_one,
    b_one,
    w_two,
    b_two,
    head,
):
    owners, capacity, width = tile_values.shape
    slots = jnp.arange(capacity, dtype=jnp.int32)
    live = slots[None, :] < tile_count[:, None]
    masked = jnp.where(live[:, :, None], tile_values, jnp.zeros_like(tile_values))
    got_values, got_block = (
        lax.all_to_all(masked, ("blk", "rep"), split_axis=0, concat_axis=0, tiled=True),
        lax.all_to_all(tile_block, ("blk", "rep"), split_axis=0, concat_axis=0, tiled=True),
    )
    weight = wide_weight(z_state, n_state)
    flat_block = got_block.reshape(-1)
    flat_values = got_values.reshape(-1, width)
    picked = jnp.take(weight, flat_block, axis=0)
    tile_logit = jnp.sum(flat_values.astype(jnp.float32) * picked, axis=1).reshape(owners, capacity)
    returned = lax.all_to_all(tile_logit, ("blk", "rep"), split_axis=0, concat_axis=0, tiled=True)
    flat_example = tile_example.reshape(-1)
    wide = jnp.zeros((dense.shape[0],), jnp.float32).at[flat_example].add(returned.reshape(-1))
    pre_one = jnp.dot(dense, w_one, preferred_element_type=jnp.float32) + b_one
    hid_one = jax.nn.silu(pre_one).astype(jnp.bfloat16)
    pre_two = jnp.dot(hid_one, w_two, preferred_element_type=jnp.float32) + b_two
    hid_two = jax.nn.silu(pre_two).astype(jnp.bfloat16)
    deep = jnp.dot(hid_two, head, preferred_element_type=jnp.float32)
    probability = jax.nn.sigmoid(wide + deep)
    residual = probability - labels.astype(jnp.float32)
    tile_residual = jnp.take(residual, flat_example).reshape(owners, capacity)
    got_residual = lax.all_to_all(
        tile_residual, ("blk", "rep"), split_axis=0, concat_axis=0, tiled=True
    )
    contrib = flat_values.astype(jnp.float32) * got_residual.reshape(-1)[:, None]
    grad_block = jnp.zeros_like(z_state).at[flat_block].add(contrib)
    n_new = n_state + grad_block * grad_block
    sigma = (jnp.sqrt(n_new) - jnp.sqrt(n_state)) / alpha_rate
    z_new = z_state + grad_block - sigma * weight
    dlogit = residual.astype(jnp.bfloat16)
    grad_head = jnp.dot(dlogit, hid_two, preferred_element_type=jnp.float32)
    d_two = (
        dlogit.astype(jnp.float32)[:, None]
        * head.astype(jnp.float32)[None, :]
        * silu_slope(pre_two)
    ).astype(jnp.bfloat16)
    grad_w_two = lax.dot_general(
        hid_one, d_two, (((0,), (0,)), ((), ())), preferred_element_type=jnp.float32
    )
    grad_b_two = jnp.sum(d_two.astype(jnp.float32), axis=0)
    back_one = lax.dot_general(
        d_two, w_two, (((1,), (1,)), ((), ())), preferred_element_type=jnp.float32
    )
    d_one = (back_one * silu_slope(pre_one)).astype(jnp.bfloat16)
    grad_w_one = lax.dot_general(
        dense, d_one, (((0,), (0,)), ((), ())), preferred_element_type=jnp.float32
    )
    grad_b_one = jnp.sum(d_one.astype(jnp.float32), axis=0)
    grad_head, grad_w_two, grad_b_two, grad_w_one, grad_b_one = lax.psum(
        (grad_head, grad_w_two, grad_b_two, grad_w_one, grad_b_one), ("blk", "rep")
    )
    return (probability, z_new, n_new, grad_w_one, grad_b_one, grad_w_two, grad_b_two, grad_head)


def solution(mesh):
    placed = (
        P(("blk", "rep"), None),
        P(("blk", "rep")),
        P(("blk", "rep"), None, None),
        P(("blk", "rep"), None),
        P(("blk", "rep"), None),
        P(("blk", "rep")),
        P(("blk", "rep"), None),
        P(("blk", "rep"), None),
        P(),
        P(),
        P(),
        P(),
        P(),
    )
    return jax.shard_map(
        per_device,
        mesh=mesh,
        in_specs=placed,
        out_specs=(
            P(("blk", "rep")),
            P(("blk", "rep"), None),
            P(("blk", "rep"), None),
            P(),
            P(),
            P(),
            P(),
            P(),
        ),
        check_vma=False,
    )
```

profile of v0, /device:TPU:1, one launch (start us, length us, event | category | flops | bytes accessed | tf_op | source)
XLA Modules:
  0.0 373.5 jit_solution(6273867925865264041)
XLA Ops:
  7.2 0.0 copy-start
  7.2 1.6 copy.30
  8.8 11.5 %all-to-all-start.1 = ((s32[128,1,64]{2,1,0:T(1,128)}), s32[128,1,64]{2,1,0:T(1,128)S(1)}, u32[]{:S(2)}, u32[]{:S(2)}) async-start(s32[128,1,64]{2,1,0:T(1,128)} %bitcast.2), calls=%async_computation.1 | async-start | bytes 131072 | tf_op jit(solution)/shard_map/all_to_all | solution.py:44
  20.3 0.7 iota_compare_fusion
  21.1 0.7 reshape.183
  21.7 0.8 copy.29
  22.6 0.1 reshape.146
  22.7 1.6 divide_select_fusion
  24.4 0.0 copy-start.5
  24.4 0.0 copy-start.8
  24.4 4.5 %broadcast_select_fusion = bf16[128,64,128]{2,1,0:T(8,128)(2,1)} fusion(bf16[128,64,128]{2,1,0:T(8,128)(2,1)} %param.15, pred[128,64]{1,0:T(8,128)(4,1)S(1)} %iota_compare_fusion), kind=kLoop, calls=%fused_computation.10 | loop fusion | flops 1048576 | bytes 4202496 | tf_op jit(solution)/shard_map/jit(_where)/select_n | solution.py:41
  29.0 2.8 multiply_convert_fusion.1
  31.7 1.4 multiply_convert_fusion.3
  33.1 0.2 fusion.3
  33.4 10.2 %all-to-all-start = ((bf16[128,64,128]{2,1,0:T(8,128)(2,1)}), bf16[128,64,128]{2,1,0:T(8,128)(2,1)}, u32[]{:S(2)}, u32[]{:S(2)}) async-start(bf16[128,64,128]{2,1,0:T(8,128)(2,1)} %broadcast_select_fusion), calls=%async_computation | async-start | bytes 4194304 | tf_op jit(solution)/shard_map/all_to_all | solution.py:43
  43.6 0.5 broadcast.153
  44.1 0.8 reduce.10
  44.9 0.1 reshape.148
  45.1 27.8 %gather_fusion = f32[8192,128]{1,0:T(8,128)} fusion(f32[1024,128]{1,0:T(8,128)S(1)} %divide_select_fusion, s32[8192]{0:T(1024)S(1)} %broadcast_clamp_fusion.1), kind=kCustom, calls=%fused_computation | custom fusion | bytes 8421376 | tf_op jit(solution)/shard_map/jit(_take)/gather | solution.py:49
  72.9 0.9 all-to-all-done
  73.8 5.4 %multiply_reduce_fusion = f32[128,64]{1,0:T(8,128)} fusion(f32[128,64,128]{2,1,0:T(8,128)} %bitcast.30, pred[128,64]{1,0:T(8,128)(4,1)S(1)} %compare_and_fusion, bf16[128,64,128]{2,1,0:T(8,128)(2,1)} %all-to-all-done), kind=kLoop, calls=%fused_computation.5 | loop fusion | flops 4186112 | bytes 6332416 | tf_op jit(solution)/shard_map/reduce_sum | solution.py:50
  79.2 8.9 %all-to-all-start.2 = ((f32[128,1,64]{2,1,0:T(1,128)}), f32[128,1,64]{2,1,0:T(1,128)S(1)}, u32[]{:S(2)}, u32[]{:S(2)}) async-start(f32[128,1,64]{2,1,0:T(1,128)} %bitcast.6), calls=%async_computation.2 | async-start | bytes 131072 | tf_op jit(solution)/shard_map/all_to_all | solution.py:51
  88.2 9.4 %all-to-all-done.2 = f32[128,1,64]{2,1,0:T(1,128)S(1)} async-done(((f32[128,1,64]{2,1,0:T(1,128)}), f32[128,1,64]{2,1,0:T(1,128)S(1)}, u32[]{:S(2)}, u32[]{:S(2)}) %all-to-all-start.2) | async-done | bytes 32800 | tf_op jit(solution)/shard_map/all_to_all | solution.py:51
  97.5 0.5 broadcast.154
  98.0 0.8 reduce.11
  98.9 0.1 reshape.171
  98.9 57.0 %scatter_fusion = f32[1024]{0:T(1024)S(1)} fusion(f32[1024]{0:T(1024)S(1)} %bitcast.29, s32[8192]{0:T(1024)S(1)} %bitcast.33, f32[8192]{0:T(1024)S(1)} %reshape.171), kind=kCustom, calls=%fused_computation.2 | custom fusion | flops 8192 | bytes 131072 | tf_op jit(solution)/shard_map/scatter-add | solution.py:53
  156.0 0.6 fusion.2
  156.6 1.8 convert_reduce_fusion.1
  158.3 2.5 fusion.4
  160.8 1.0 convert_reduce_fusion
  161.9 2.6 convolution_bitcast_fusion
  164.5 32.9 %gather_fusion.1 = f32[8192]{0:T(1024)S(1)} fusion(f32[1024]{0:T(1024)S(1)} %get-tuple-element.41, s32[8192]{0:T(1024)S(1)} %broadcast_clamp_fusion), kind=kCustom, calls=%fused_computation.1 | custom fusion | bytes 98304 | tf_op jit(solution)/shard_map/jit(_take)/gather | solution.py:61
  197.4 0.1 gather.15
  197.4 0.7 and_select_fusion
  198.1 4.6 %all-to-all-start.3 = ((f32[128,1,64]{2,1,0:T(1,128)}), f32[128,1,64]{2,1,0:T(1,128)S(1)}, u32[]{:S(2)}, u32[]{:S(2)}) async-start(f32[128,1,64]{2,1,0:T(1,128)} %bitcast.9), calls=%async_computation.3 | async-start | bytes 131072 | tf_op jit(solution)/shard_map/all_to_all | solution.py:62
  202.7 0.0 all-reduce.4.cloned.1.call-start
  202.8 0.2 fusion.5
  202.9 0.5 all-reduce.4.cloned.1.call-update
  203.4 67.4 %all-reduce = (f32[512]{0:T(512)}, f32[256]{0:T(256)}, f32[256]{0:T(256)}) all-reduce(f32[512]{0:T(512)S(1)} %get-tuple-element.49, f32[256]{0:T(256)S(1)} %get-tuple-element.37, f32[256]{0:T(256)S(1)} %bitcast.36), channel_id=1, replica_groups=mesh['blk'=16,'rep'=8] {'blk','rep'}, use_global_device_ids=true, to_apply=%region_5.6 | all-reduce | flops 1024 | bytes 8192 | tf_op jit(solution)/shard_map/psum | solution.py:89
  270.9 0.8 reduce.12
  271.7 0.1 mul.66
  271.8 3.9 %bitcast_multiply_fusion = f32[8192,128]{1,0:T(8,128)} fusion(f32[8192]{0:T(1024)S(1)} %mul.66, bf16[128,64,128]{2,1,0:T(8,128)(2,1)} %all-to-all-done), kind=kLoop, calls=%fused_computation.4 | loop fusion | flops 2097152 | bytes 6324224 | tf_op jit(solution)/shard_map/mul | solution.py:65
  275.7 45.1 %scatter_custom_fusion.1 = f32[1024,128]{1,0:T(8,128)} fusion(s32[8192]{0:T(1024)S(1)} %bitcast.35, f32[8192,128]{1,0:T(8,128)} %bitcast_multiply_fusion, f32[]{:T(128)} %constant.32.clone.1), kind=kCustom, calls=%fused_computation.21 | custom fusion | flops 1048576 | bytes 524800 | tf_op jit(solution)/shard_map/scatter-add | solution.py:66
  320.7 2.7 multiply_subtract_fusion
  323.4 39.5 %all-reduce.4.cloned.1.call-done = (f32[1024,512]{0,1:T(8,128)}, f32[512,256]{1,0:T(8,128)}) async-done(((f32[1024,512]{0,1:T(8,128)}, f32[512,256]{1,0:T(8,128)}), (f32[1024,512]{0,1:T(8,128)}, f32[512,256]{1,0:T(8,128)})) %all-reduce.4.cloned.1.call-update) | async-done | bytes 2621456 | tf_op jit(solution)/shard_map/psum | solution.py:89
  362.9 2.9 copy.35
  365.8 0.8 copy.39
  (32 shorter events, 0.2 us)
Async XLA Ops:
  7.2 21.8 %copy-start = (bf16[1024,1024]{1,0:T(8,128)(2,1)S(1)}, bf16[1024,1024]{1,0:T(8,128)(2,1)}, u32[]{:S(2)}) copy-start(bf16[1024,1024]{1,0:T(8,128)(2,1)} %param.13) | copy-start | bytes 6291460
  8.8 24.6 %all-to-all-start.1 = ((s32[128,1,64]{2,1,0:T(1,128)}), s32[128,1,64]{2,1,0:T(1,128)S(1)}, u32[]{:S(2)}, u32[]{:S(2)}) async-start(s32[128,1,64]{2,1,0:T(1,128)} %bitcast.2), calls=%async_computation.1 | async-start | bytes 131072 | tf_op jit(solution)/shard_map/all_to_all | solution.py:44
  24.4 4.6 %copy-start.5 = (bf16[1024,512]{1,0:T(8,128)(2,1)S(1)}, bf16[1024,512]{1,0:T(8,128)(2,1)}, u32[]{:S(2)}) copy-start(bf16[1024,512]{1,0:T(8,128)(2,1)} %param.21) | copy-start | bytes 3145732
  24.4 4.5 %copy-start.8 = (f32[512]{0:T(512)S(1)}, f32[512]{0:T(512)}, u32[]{:S(2)}) copy-start(f32[512]{0:T(512)} %param.22) | copy-start | bytes 6148
  28.9 2.8 copy-start.6
  28.9 2.8 copy-start.9
  31.7 1.4 copy-start.11
  33.4 40.4 %all-to-all-start = ((bf16[128,64,128]{2,1,0:T(8,128)(2,1)}), bf16[128,64,128]{2,1,0:T(8,128)(2,1)}, u32[]{:S(2)}, u32[]{:S(2)}) async-start(bf16[128,64,128]{2,1,0:T(8,128)(2,1)} %broadcast_select_fusion), calls=%async_computation | async-start | bytes 4194304 | tf_op jit(solution)/shard_map/all_to_all | solution.py:43
  73.8 14.3 %copy-start.10 = (bf16[256]{0:T(256)(128)(2,1)S(1)}, bf16[256]{0:T(256)(128)(2,1)}, u32[]{:S(2)}) copy-start(bf16[256]{0:T(256)(128)(2,1)} %param.25) | copy-start | bytes 1540
  79.2 18.3 %all-to-all-start.2 = ((f32[128,1,64]{2,1,0:T(1,128)}), f32[128,1,64]{2,1,0:T(1,128)S(1)}, u32[]{:S(2)}, u32[]{:S(2)}) async-start(f32[128,1,64]{2,1,0:T(1,128)} %bitcast.6), calls=%async_computation.2 | async-start | bytes 131072 | tf_op jit(solution)/shard_map/all_to_all | solution.py:51
  98.9 57.0 %copy-start.4 = (s32[1024]{0:T(1024)S(1)}, s32[1024]{0:T(1024)}, u32[]{:S(2)}) copy-start(s32[1024]{0:T(1024)} %param.14) | copy-start | bytes 12292
  156.0 4.9 %copy-start.7 = (bf16[512,256]{1,0:T(8,128)(2,1)S(1)}, bf16[512,256]{1,0:T(8,128)(2,1)}, u32[]{:S(2)}) copy-start(bf16[512,256]{1,0:T(8,128)(2,1)} %param.23) | copy-start | bytes 786436
  156.0 4.9 %copy-start.12 = (f32[1024,512]{1,0:T(8,128)S(1)}, f32[1024,512]{1,0:T(8,128)}, u32[]{:S(2)}) copy-start(f32[1024,512]{1,0:T(8,128)} %get-tuple-element.46) | copy-start | bytes 6291460
  198.1 72.8 %all-to-all-start.3 = ((f32[128,1,64]{2,1,0:T(1,128)}), f32[128,1,64]{2,1,0:T(1,128)S(1)}, u32[]{:S(2)}, u32[]{:S(2)}) async-start(f32[128,1,64]{2,1,0:T(1,128)} %bitcast.9), calls=%async_computation.3 | async-start | bytes 131072 | tf_op jit(solution)/shard_map/all_to_all | solution.py:62
  202.7 160.2 %all-reduce.4.cloned.1.call-start = ((), (), s32[]{:S(2)}) async-start(), calls=%async_computation.4 | async-start | bytes 5242880 | tf_op jit(solution)/shard_map/psum | solution.py:89
  271.8 49.0 %copy-start.1 = (f32[1024,128]{1,0:T(8,128)S(1)}, f32[1024,128]{1,0:T(8,128)}, u32[]{:S(2)}) copy-start(f32[1024,128]{1,0:T(8,128)} %param.19) | copy-start | bytes 1572868
  271.8 49.0 %copy-start.2 = (f32[1024,128]{1,0:T(8,128)S(1)}, f32[1024,128]{1,0:T(8,128)}, u32[]{:S(2)}) copy-start(f32[1024,128]{1,0:T(8,128)} %param.20) | copy-start | bytes 1572868
  362.9 2.9 copy-start.3
Sparse Core Ops, SparseCore 0:
  209.1 153.7 all-reduce.3
where the time goes:
time: 374 us; the launch traced here: 373 us
  other arithmetic  127 us (34%)
  local copies, waits for them, and re-layouts  69 us (18%)
  blocking collectives  67.4 us (18%)
  waiting for transfers between devices  50.3 us (13%)
  starting transfers between devices  35.3 us (9%)
  between operations  14.3 us (4%)
  matrix products  10.7 us (3%)
    psum x1, blocking collectives, per_device(): lax.psum((grad_head, grad_w_two, grad_b_two, grad_w_one, grad_b_one), ('b...  67.4 us
    scatter-add x1, other arithmetic, per_device(): jnp.zeros((dense.shape[0],), jnp.float32).at[flat_example]  57 us
    scatter-add x1, other arithmetic, per_device(): grad_block = jnp.zeros_like(z_state).at[flat_block].add(contrib)  45.1 us
    psum x1, waiting for transfers between devices, per_device(): lax.psum((grad_head, grad_w_two, grad_b_two, grad_w_one, grad_b_one), ('b...  39.5 us
    gather x2, local copies, waits for them, and re-layouts, per_device(): tile_residual = jnp.take(residual, flat_example).reshape(owners, capacity)  32.9 us
    gather x1, local copies, waits for them, and re-layouts, per_device(): picked = jnp.take(weight, flat_block, axis=0)  27.8 us
    all_to_all x1, starting transfers between devices, per_device(): lax.all_to_all(tile_block, ('blk', 'rep'), split_axis=0, concat_axis=0, t...  11.5 us
    all_to_all x1, starting transfers between devices, per_device(): lax.all_to_all(masked, ('blk', 'rep'), split_axis=0, concat_axis=0, tiled...  10.2 us
  transfers between devices with their start and end apart: 5, of which 3 were waited for; matrix products, arithmetic and copies ran while one was open for 25% of the time, Pallas kernels for 0%

commit v1 on v0

--- a/solution.py
+++ b/solution.py
@@ -87,7 +87,7 @@
     )
     grad_b_one = jnp.sum(d_one.astype(jnp.float32), axis=0)
     grad_head, grad_w_two, grad_b_two, grad_w_one, grad_b_one = lax.psum(
-        (grad_head, grad_w_two, grad_b_two, grad_w_one, grad_b_one), ("blk", "rep")
+        lax.psum((grad_head, grad_w_two, grad_b_two, grad_w_one, grad_b_one), "blk"), "rep"
     )
     return (probability, z_new, n_new, grad_w_one, grad_b_one, grad_w_two, grad_b_two, grad_head)
 

time: 374 us -> 333 us (0.89)
  waiting for transfers between devices: 50.3 us -> 21.4 us
  blocking collectives: 67.4 us -> 54.7 us
    psum x1 -> x2, waiting for transfers between devices: 39.5 us -> 11.4 us  [the longest x1 11.4 us: per_device(): lax.psum(lax.psum((grad_head, grad_w_two, grad_b_two, grad_w_one, grad_b_...]
    psum x1 -> x2, blocking collectives: 67.4 us -> 54.7 us  [the longest x1 34.2 us: per_device(): lax.psum((grad_head, grad_w_two, grad_b_two, grad_w_one, grad_b_one), 'blk')]
  transfers between devices with their start and end apart: 5 -> 6, of which waited for: 3 -> 3; matrix products, arithmetic and copies ran while one was open for 25% -> 38% of each run, Pallas kernels for 0% -> 0%
where the time goes in v1:
time: 333 us; the launch traced here: 331 us
  other arithmetic  125 us (38%)
  local copies, waits for them, and re-layouts  68.7 us (21%)
  blocking collectives  54.7 us (16%)
  starting transfers between devices  35.3 us (11%)
  waiting for transfers between devices  21.4 us (6%)
  between operations  14.3 us (4%)
  matrix products  10.9 us (3%)
    scatter-add x1, other arithmetic, per_device(): jnp.zeros((dense.shape[0],), jnp.float32).at[flat_example]  57 us
    scatter-add x1, other arithmetic, per_device(): grad_block = jnp.zeros_like(z_state).at[flat_block].add(contrib)  45.1 us
    psum x1, blocking collectives, per_device(): lax.psum((grad_head, grad_w_two, grad_b_two, grad_w_one, grad_b_one), 'blk')  34.2 us
    gather x2, local copies, waits for them, and re-layouts, per_device(): tile_residual = jnp.take(residual, flat_example).reshape(owners, capacity)  33 us
    gather x1, local copies, waits for them, and re-layouts, per_device(): picked = jnp.take(weight, flat_block, axis=0)  27.8 us
    psum x1, blocking collectives, per_device(): lax.psum(lax.psum((grad_head, grad_w_two, grad_b_two, grad_w_one, grad_b_...  20.4 us
    all_to_all x1, starting transfers between devices, per_device(): lax.all_to_all(tile_block, ('blk', 'rep'), split_axis=0, concat_axis=0, t...  11.5 us
    psum x1, waiting for transfers between devices, per_device(): lax.psum(lax.psum((grad_head, grad_w_two, grad_b_two, grad_w_one, grad_b_...  11.4 us
  transfers between devices with their start and end apart: 6, of which 3 were waited for; matrix products, arithmetic and copies ran while one was open for 38% of the time, Pallas kernels for 0%

profile of v1, /device:TPU:1, one launch (start us, length us, event | category | flops | bytes accessed | tf_op | source)
XLA Modules:
  0.0 330.7 jit_solution(10072336600690655035)
XLA Ops:
  7.2 1.6 copy.30
  8.8 11.5 %all-to-all-start.1 = ((s32[128,1,64]{2,1,0:T(1,128)}), s32[128,1,64]{2,1,0:T(1,128)S(1)}, u32[]{:S(2)}, u32[]{:S(2)}) async-start(s32[128,1,64]{2,1,0:T(1,128)} %bitcast.2), calls=%async_computation.1 | async-start | bytes 131072 | tf_op jit(solution)/shard_map/all_to_all | solution.py:44
  20.3 0.7 iota_compare_fusion
  21.1 0.8 copy.29
  21.9 0.1 reshape.146
  22.1 4.5 %broadcast_select_fusion = bf16[128,64,128]{2,1,0:T(8,128)(2,1)} fusion(bf16[128,64,128]{2,1,0:T(8,128)(2,1)} %param.15, pred[128,64]{1,0:T(8,128)(4,1)S(1)} %iota_compare_fusion), kind=kLoop, calls=%fused_computation.10 | loop fusion | flops 1048576 | bytes 4202496 | tf_op jit(solution)/shard_map/jit(_where)/select_n | solution.py:41
  26.7 2.8 multiply_convert_fusion.1
  29.5 1.6 multiply_convert_fusion.3
  31.1 0.3 copy-done.2
  31.4 0.4 divide_select_fusion
  31.9 10.2 %all-to-all-start = ((bf16[128,64,128]{2,1,0:T(8,128)(2,1)}), bf16[128,64,128]{2,1,0:T(8,128)(2,1)}, u32[]{:S(2)}, u32[]{:S(2)}) async-start(bf16[128,64,128]{2,1,0:T(8,128)(2,1)} %broadcast_select_fusion), calls=%async_computation | async-start | bytes 4194304 | tf_op jit(solution)/shard_map/all_to_all | solution.py:43
  42.1 0.5 broadcast.153
  42.6 0.8 reduce.10
  43.4 0.1 reshape.148
  43.6 27.8 %gather_fusion = f32[8192,128]{1,0:T(8,128)} fusion(f32[1024,128]{1,0:T(8,128)S(1)} %divide_select_fusion, s32[8192]{0:T(1024)S(1)} %broadcast_clamp_fusion.1), kind=kCustom, calls=%fused_computation | custom fusion | bytes 8421376 | tf_op jit(solution)/shard_map/jit(_take)/gather | solution.py:49
  71.4 0.9 all-to-all-done
  72.3 5.5 %multiply_reduce_fusion = f32[128,64]{1,0:T(8,128)} fusion(f32[128,64,128]{2,1,0:T(8,128)} %bitcast.30, pred[128,64]{1,0:T(8,128)(4,1)S(1)} %compare_and_fusion, bf16[128,64,128]{2,1,0:T(8,128)(2,1)} %all-to-all-done), kind=kLoop, calls=%fused_computation.5 | loop fusion | flops 4186112 | bytes 6332416 | tf_op jit(solution)/shard_map/reduce_sum | solution.py:50
  77.8 8.9 %all-to-all-start.2 = ((f32[128,1,64]{2,1,0:T(1,128)}), f32[128,1,64]{2,1,0:T(1,128)S(1)}, u32[]{:S(2)}, u32[]{:S(2)}) async-start(f32[128,1,64]{2,1,0:T(1,128)} %bitcast.6), calls=%async_computation.2 | async-start | bytes 131072 | tf_op jit(solution)/shard_map/all_to_all | solution.py:51
  86.7 0.0 all-reduce.7.cloned.1.call-start
  86.7 0.2 fusion.3
  87.0 9.1 %all-to-all-done.2 = f32[128,1,64]{2,1,0:T(1,128)S(1)} async-done(((f32[128,1,64]{2,1,0:T(1,128)}), f32[128,1,64]{2,1,0:T(1,128)S(1)}, u32[]{:S(2)}, u32[]{:S(2)}) %all-to-all-start.2) | async-done | bytes 32800 | tf_op jit(solution)/shard_map/all_to_all | solution.py:51
  96.1 0.5 broadcast.154
  96.6 0.8 reduce.11
  97.4 0.1 reshape.171
  97.5 57.0 %scatter_fusion = f32[1024]{0:T(1024)S(1)} fusion(f32[1024]{0:T(1024)S(1)} %bitcast.29, s32[8192]{0:T(1024)S(1)} %bitcast.32, f32[8192]{0:T(1024)S(1)} %reshape.171), kind=kCustom, calls=%fused_computation.2 | custom fusion | flops 8192 | bytes 131072 | tf_op jit(solution)/shard_map/scatter-add | solution.py:53
  154.5 0.6 fusion.2
  155.2 1.8 convert_reduce_fusion.1
  156.9 2.5 fusion.4
  159.4 1.0 convert_reduce_fusion
  160.4 2.6 convolution_bitcast_fusion
  163.0 0.0 all-reduce.7.cloned.1.call-update
  163.1 32.9 %gather_fusion.1 = f32[8192]{0:T(1024)S(1)} fusion(f32[1024]{0:T(1024)S(1)} %get-tuple-element.46, s32[8192]{0:T(1024)S(1)} %broadcast_clamp_fusion), kind=kCustom, calls=%fused_computation.1 | custom fusion | bytes 98304 | tf_op jit(solution)/shard_map/jit(_take)/gather | solution.py:61
  196.0 0.1 gather.15
  196.1 0.6 and_select_fusion
  196.7 4.6 %all-to-all-start.3 = ((f32[128,1,64]{2,1,0:T(1,128)}), f32[128,1,64]{2,1,0:T(1,128)S(1)}, u32[]{:S(2)}, u32[]{:S(2)}) async-start(f32[128,1,64]{2,1,0:T(1,128)} %bitcast.9), calls=%async_computation.3 | async-start | bytes 131072 | tf_op jit(solution)/shard_map/all_to_all | solution.py:62
  201.3 0.0 all-reduce.9.cloned.1.call-start
  201.4 0.2 fusion.5
  201.6 34.2 %all-reduce = (f32[512]{0:T(512)S(1)}, f32[256]{0:T(256)S(1)}, f32[256]{0:T(256)S(1)}) all-reduce(f32[512]{0:T(512)S(1)} %get-tuple-element.54, f32[256]{0:T(256)S(1)} %get-tuple-element.42, f32[256]{0:T(256)S(1)} %bitcast.36), channel_id=1, replica_groups=mesh['blk'=16,'rep'=8] {'blk'}, use_global_device_ids=true, to_apply=%region_6.7 | all-reduce | flops 1024 | bytes 8192 | tf_op jit(solution)/shard_map/psum | solution.py:90
  235.8 20.4 %all-reduce.2 = (f32[512]{0:T(512)}, f32[256]{0:T(256)}, f32[256]{0:T(256)}) all-reduce(f32[512]{0:T(512)S(1)} %get-tuple-element.32, f32[256]{0:T(256)S(1)} %get-tuple-element.33, f32[256]{0:T(256)S(1)} %get-tuple-element.34), channel_id=1, replica_groups=mesh['blk'=16,'rep'=8] {'rep'}, use_global_device_ids=true, to_apply=%region_7.8 | all-reduce | flops 1024 | bytes 8192 | tf_op jit(solution)/shard_map/psum | solution.py:89
  256.2 0.8 reduce.12
  257.0 0.1 mul.66
  257.1 0.0 all-reduce.9.cloned.1.call-update
  257.1 3.8 %bitcast_multiply_fusion = f32[8192,128]{1,0:T(8,128)} fusion(f32[8192]{0:T(1024)S(1)} %mul.66, bf16[128,64,128]{2,1,0:T(8,128)(2,1)} %all-to-all-done), kind=kLoop, calls=%fused_computation.4 | loop fusion | flops 2097152 | bytes 6324224 | tf_op jit(solution)/shard_map/mul | solution.py:65
  261.0 45.1 %scatter_custom_fusion.1 = f32[1024,128]{1,0:T(8,128)} fusion(s32[8192]{0:T(1024)S(1)} %bitcast.35, f32[8192,128]{1,0:T(8,128)} %bitcast_multiply_fusion, f32[]{:T(128)} %constant.32.clone.1), kind=kCustom, calls=%fused_computation.21 | custom fusion | flops 1048576 | bytes 524800 | tf_op jit(solution)/shard_map/scatter-add | solution.py:66
  306.1 2.7 multiply_subtract_fusion
  308.7 11.4 %all-reduce.9.cloned.1.call-done = (f32[1024,512]{0,1:T(8,128)}, f32[512,256]{1,0:T(8,128)}) async-done(((f32[1024,512]{0,1:T(8,128)}, f32[512,256]{1,0:T(8,128)}), (f32[1024,512]{0,1:T(8,128)}, f32[512,256]{1,0:T(8,128)})) %all-reduce.9.cloned.1.call-update) | async-done | bytes 2621456 | tf_op jit(solution)/shard_map/psum | solution.py:89
  320.1 2.9 copy.35
  323.1 0.8 copy.41
  (40 shorter events, 0.2 us)
Async XLA Ops:
  7.2 19.5 %copy-start = (bf16[1024,1024]{1,0:T(8,128)(2,1)S(1)}, bf16[1024,1024]{1,0:T(8,128)(2,1)}, u32[]{:S(2)}) copy-start(bf16[1024,1024]{1,0:T(8,128)(2,1)} %param.13) | copy-start | bytes 6291460
  8.8 23.1 %all-to-all-start.1 = ((s32[128,1,64]{2,1,0:T(1,128)}), s32[128,1,64]{2,1,0:T(1,128)S(1)}, u32[]{:S(2)}, u32[]{:S(2)}) async-start(s32[128,1,64]{2,1,0:T(1,128)} %bitcast.2), calls=%async_computation.1 | async-start | bytes 131072 | tf_op jit(solution)/shard_map/all_to_all | solution.py:44
  22.1 4.6 %copy-start.7 = (bf16[1024,512]{1,0:T(8,128)(2,1)S(1)}, bf16[1024,512]{1,0:T(8,128)(2,1)}, u32[]{:S(2)}) copy-start(bf16[1024,512]{1,0:T(8,128)(2,1)} %param.21) | copy-start | bytes 3145732
  22.1 4.6 %copy-start.10 = (f32[512]{0:T(512)S(1)}, f32[512]{0:T(512)}, u32[]{:S(2)}) copy-start(f32[512]{0:T(512)} %param.22) | copy-start | bytes 6148
  26.7 2.8 copy-start.8
  26.7 2.8 copy-start.11
  29.5 1.6 copy-start.13
  29.5 1.6 copy-start.1
  29.5 2.0 copy-start.2
  29.5 2.4 copy-start.12
  31.9 40.4 %all-to-all-start = ((bf16[128,64,128]{2,1,0:T(8,128)(2,1)}), bf16[128,64,128]{2,1,0:T(8,128)(2,1)}, u32[]{:S(2)}, u32[]{:S(2)}) async-start(bf16[128,64,128]{2,1,0:T(8,128)(2,1)} %broadcast_select_fusion), calls=%async_computation | async-start | bytes 4194304 | tf_op jit(solution)/shard_map/all_to_all | solution.py:43
  72.3 14.4 %copy-start.4 = (bf16[1024,256]{1,0:T(8,128)(2,1)S(1)}, bf16[1024,256]{1,0:T(8,128)(2,1)}, u32[]{:S(2)}) copy-start(bf16[1024,256]{1,0:T(8,128)(2,1)} %get-tuple-element.52) | copy-start | bytes 1572868
  77.8 18.3 %all-to-all-start.2 = ((f32[128,1,64]{2,1,0:T(1,128)}), f32[128,1,64]{2,1,0:T(1,128)S(1)}, u32[]{:S(2)}, u32[]{:S(2)}) async-start(f32[128,1,64]{2,1,0:T(1,128)} %bitcast.6), calls=%async_computation.2 | async-start | bytes 131072 | tf_op jit(solution)/shard_map/all_to_all | solution.py:51
  86.7 170.4 %all-reduce.7.cloned.1.call-start = ((), (), s32[]{:S(2)}) async-start(), calls=%async_computation.4 | async-start | bytes 5242880 | tf_op jit(solution)/shard_map/psum | solution.py:90
  97.5 57.0 %copy-start.6 = (s32[1024]{0:T(1024)S(1)}, s32[1024]{0:T(1024)}, u32[]{:S(2)}) copy-start(s32[1024]{0:T(1024)} %param.14) | copy-start | bytes 12292
  154.5 4.9 %copy-start.9 = (bf16[512,256]{1,0:T(8,128)(2,1)S(1)}, bf16[512,256]{1,0:T(8,128)(2,1)}, u32[]{:S(2)}) copy-start(bf16[512,256]{1,0:T(8,128)(2,1)} %param.23) | copy-start | bytes 786436
  154.5 4.9 %copy-start.14 = (f32[1024,512]{1,0:T(8,128)S(1)}, f32[1024,512]{1,0:T(8,128)}, u32[]{:S(2)}) copy-start(f32[1024,512]{1,0:T(8,128)} %get-tuple-element.51) | copy-start | bytes 6291460
  196.7 59.5 %all-to-all-start.3 = ((f32[128,1,64]{2,1,0:T(1,128)}), f32[128,1,64]{2,1,0:T(1,128)S(1)}, u32[]{:S(2)}, u32[]{:S(2)}) async-start(f32[128,1,64]{2,1,0:T(1,128)} %bitcast.9), calls=%async_computation.3 | async-start | bytes 131072 | tf_op jit(solution)/shard_map/all_to_all | solution.py:62
  201.3 118.8 %all-reduce.9.cloned.1.call-start = ((), (), s32[]{:S(2)}) async-start(), calls=%async_computation.5 | async-start | bytes 5242880 | tf_op jit(solution)/shard_map/psum | solution.py:89
  257.1 48.9 %copy-start.3 = (f32[1024,128]{1,0:T(8,128)S(1)}, f32[1024,128]{1,0:T(8,128)}, u32[]{:S(2)}) copy-start(f32[1024,128]{1,0:T(8,128)} %param.20) | copy-start | bytes 1572868
  320.1 2.9 copy-start.5
Sparse Core Ops, SparseCore 0:
  163.2 89.0 all-reduce.6
  257.3 62.8 all-reduce.8
